TPU v7x, 128 devices: a whole 4x4x4 slice. The times are simulated.
128 devices in a mesh: dp: 16 (over x, z_lo, core), tensor: 8 (over z_hi, y).
Axes of the slice: x: 4, y: 4, z: 4 (z_hi: 2, z_lo: 2; z = z_hi * 2 + z_lo), core: 2. Of those that a mesh axis runs over, the one named last changes fastest.
Arguments:
- inputs: bfloat16 [4096, 4096], P('dp', 'tensor'), may hold values from -6 to 6
- gate_pre: bfloat16 [4096, 14336], P('dp', 'tensor'), may hold values from -9 to 9
- up_pre: bfloat16 [4096, 14336], P('dp', 'tensor'), may hold values from -6 to 6
- out_grad: bfloat16 [4096, 4096], P('dp', 'tensor'), may hold values from -0.09375 to 0.09375
- down_weight: bfloat16 [14336, 4096], P('tensor'), may hold values from -0.09375 to 0.09375
Outputs:
- gate_wgrad: bfloat16 [4096, 14336], P('dp', 'tensor')
- up_wgrad: bfloat16 [4096, 14336], P('dp', 'tensor')
- in_cov: float32 [4096, 1024], P(('dp', 'tensor'))
- gate_cov: float32 [8, 1792, 896], P('tensor', 'dp')
- up_cov: float32 [8, 1792, 896], P('tensor', 'dp')
All inputs are finite; a program needn't handle non-finite values.
Results may differ from a plain program's by a relative error of at most 0.014.
Values may be sent and summed in bfloat16 or wider, within the bound.
A program may use at most 192 MiB of HBM per device.

v0:
```python
import jax
import jax.numpy as jnp
from jax import lax
from jax.sharding import PartitionSpec as P

BLK = 1024
HBLK = 896


def sent_together(arrays, axis, dim, along):
    both = jnp.concatenate(arrays, axis=along)
    whole, at, outs = (lax.all_gather(both, axis, axis=dim, tiled=True), 0, [])
    for a in arrays:
        outs.append(lax.slice_in_dim(whole, at, at + a.shape[along], axis=along))
        at += a.shape[along]
    return tuple(outs)


def split_up(x, dim, count):
    shape = x.shape
    tiles = x.reshape(*shape[:dim], count, shape[dim] // count, *shape[dim + 1 :])
    return jnp.moveaxis(tiles, dim, 0)


def summed_on_arrival(x, axis, dim):
    tiles = split_up(x, dim, lax.axis_size(axis))
    arrived = lax.all_to_all(tiles, axis, split_axis=0, concat_axis=0, tiled=True)
    return arrived.astype(jnp.float32).sum(axis=0)


def inner(left, right):
    return lax.dot_general(
        left, right, (((0,), (0,)), ((), ())), preferred_element_type=jnp.float32
    )


def on_device(inputs, gate_pre, up_pre, out_grad, down_weight):
    dp_count = lax.axis_size("dp")
    tp_count = lax.axis_size("tensor")
    dp_index = lax.axis_index("dp")
    tp_index = lax.axis_index("tensor")
    inputs_full, grad_full = sent_together((inputs, out_grad), "tensor", 1, 0)
    tok_rows = inputs_full.shape[0]
    width = inputs_full.shape[1]
    total_tokens = tok_rows * dp_count
    own_width = width // dp_count
    cov_rows = width // (dp_count * tp_count)
    block_count = width // BLK
    repeated = jnp.repeat(
        inputs_full.reshape(tok_rows, block_count, BLK), dp_count // block_count, axis=1
    )
    split = inputs_full.reshape(tok_rows, dp_count, own_width)
    x_owned = lax.all_to_all(split, "dp", split_axis=1, concat_axis=0, tiled=True).reshape(
        total_tokens, own_width
    )
    picked = inputs_full.reshape(tok_rows, dp_count, tp_count, cov_rows)
    picked = lax.dynamic_index_in_dim(picked, tp_index, 2, keepdims=False)
    term = jnp.einsum("tdr,tdb->drb", picked, repeated, preferred_element_type=jnp.float32)
    in_cov = summed_on_arrival(term.astype(jnp.bfloat16), "dp", 0)[0] / total_tokens
    hidden_grad = lax.dot_general(
        grad_full, down_weight, (((1,), (1,)), ((), ())), preferred_element_type=jnp.float32
    )
    gate = gate_pre.astype(jnp.float32)
    up = up_pre.astype(jnp.float32)
    sig = jax.nn.sigmoid(gate)
    gate_grad = (hidden_grad * up * sig * (1.0 + gate * (1.0 - sig))).astype(jnp.bfloat16)
    up_grad = (hidden_grad * gate * sig).astype(jnp.bfloat16)
    hidden = gate_grad.shape[1]
    hid_rows = hidden // dp_count
    row_start = dp_index * hid_rows
    block_start = row_start // HBLK * HBLK

    def accumulate_one(piece):
        wgrad = inner(x_owned, piece)
        own_cols = lax.dynamic_slice_in_dim(piece, row_start, hid_rows, 1)
        block_cols_h = lax.dynamic_slice_in_dim(piece, block_start, HBLK, 1)
        factor = inner(own_cols, block_cols_h)
        return (wgrad, factor)

    gate_sums = accumulate_one(lax.all_gather(gate_grad, "dp", axis=0, tiled=True))
    up_sums = accumulate_one(lax.all_gather(up_grad, "dp", axis=0, tiled=True))
    gate_wgrad = gate_sums[0].astype(jnp.bfloat16)
    up_wgrad = up_sums[0].astype(jnp.bfloat16)
    gate_cov = gate_sums[1].reshape(1, hid_rows, HBLK)
    up_cov = up_sums[1].reshape(1, hid_rows, HBLK)
    return (gate_wgrad, up_wgrad, in_cov, gate_cov, up_cov)


def solution(mesh):
    placed = (
        P("dp", "tensor"),
        P("dp", "tensor"),
        P("dp", "tensor"),
        P("dp", "tensor"),
        P("tensor", None),
    )
    return jax.shard_map(
        on_device,
        mesh=mesh,
        in_specs=placed,
        out_specs=(
            P("dp", "tensor"),
            P("dp", "tensor"),
            P(("dp", "tensor"), None),
            P("tensor", "dp", None),
            P("tensor", "dp", None),
        ),
        check_vma=False,
    )
```

profile of v0, /device:TPU:7, one launch (start us, length us, event | category | flops | bytes accessed | tf_op | source)
XLA Modules:
  0.0 318.3 jit_solution(9122356042220366269)
XLA Ops:
  7.2 0.0 copy-start.4
  7.2 0.0 copy-start.3
  7.2 0.0 all-gather.4.cloned.1.call-start
  7.2 1.2 copy.19
  8.4 1.1 copy.20
  9.5 0.8 pad_maximum_fusion
  10.4 0.0 all-gather.4.cloned.1.call-update
  10.4 0.0 all-gather.6.cloned.1.call-start
  10.4 74.1 %all-gather.4.cloned.1.call-done = bf16[512,4096]{0,1:T(8,128)(2,1)} async-done(((bf16[512,512]{0,1:T(8,128)(2,1)}), bf16[512,4096]{0,1:T(8,128)(2,1)}) %all-gather.4.cloned.1.call-update) | async-done | bytes 4194320 | tf_op jit(solution)/shard_map/all_gather | solution.py:12
  84.5 0.0 copy-done.4
  84.5 0.0 copy-done.3
  84.5 11.7 %fusion.13 = (bf16[256,1792]{1,0:T(8,128)(2,1)}, bf16[256,1792]{1,0:T(8,128)(2,1)}) fusion(bf16[256,1792]{1,0:T(8,128)(2,1)S(1)} %copy-done.3, bf16[256,1792]{1,0:T(8,128)(2,1)S(1)} %copy-done.4, bf16[1792,4096]{1,0:T(8,128)(2,1)} %param.9, bf16[512,4096]{0,1:T(8,128)(2,1)} %all-gather.4.cloned.1.call-done), kind=kOutput, calls=%fused_computation.19 | convolution fusion | flops 3764977664 | bytes 20447232 | tf_op jit(solution)/shard_map/dot_general | solution.py:60
  96.2 0.0 all-gather.6.cloned.1.call-update
  96.2 0.0 all-gather.8.cloned.1.call-start
  96.3 0.7 all-gather.8.cloned.1.call-update
  97.0 3.0 slice.8
  100.0 3.0 copy.22
  103.0 1.1 broadcast_in_dim.3
  104.2 2.5 fusion.14
  106.7 30.6 %all_to_all.20 = bf16[16,1,32,1024]{3,2,1,0:T(8,128)(2,1)S(1)} all-to-all(bf16[16,1,32,1024]{3,2,1,0:T(8,128)(2,1)S(1)} %fusion.14), channel_id=1, replica_groups=mesh['dp'=16,'tensor'=8] {'dp'}, dimensions={0} | all-to-all | bytes 2097152 | tf_op jit(solution)/shard_map/all_to_all | solution.py:27
  137.3 5.5 %all-to-all-start = ((bf16[256,16,256]{0,2,1:T(8,128)(2,1)}), bf16[256,16,256]{0,2,1:T(8,128)(2,1)S(1)}, u32[]{:S(2)}, u32[]{:S(2)}) async-start(bf16[256,16,256]{0,2,1:T(8,128)(2,1)} %bitcast), calls=%async_computation | async-start | bytes 4194304 | tf_op jit(solution)/shard_map/all_to_all | solution.py:53
  142.8 0.2 convert_reduce_fusion
  143.0 0.7 broadcast_multiply_fusion
  143.7 46.8 %all-to-all-done = bf16[256,16,256]{0,2,1:T(8,128)(2,1)S(1)} async-done(((bf16[256,16,256]{0,2,1:T(8,128)(2,1)}), bf16[256,16,256]{0,2,1:T(8,128)(2,1)S(1)}, u32[]{:S(2)}, u32[]{:S(2)}) %all-to-all-start) | async-done | bytes 2097184 | tf_op jit(solution)/shard_map/all_to_all | solution.py:53
  190.5 0.0 copy-start.2
  190.5 1.3 copy-done.2
  191.8 2.9 copy.21
  194.7 15.5 %all-gather.6.cloned.1.call-done = bf16[4096,1792]{1,0:T(8,128)(2,1)} async-done(((bf16[256,1792]{1,0:T(8,128)(2,1)}), bf16[4096,1792]{1,0:T(8,128)(2,1)}) %all-gather.6.cloned.1.call-update) | async-done | bytes 14680080 | tf_op jit(solution)/shard_map/all_gather | solution.py:80
  210.3 8.3 %convolution_convert_fusion.1 = bf16[256,1792]{1,0:T(8,128)(2,1)} fusion(bf16[4096,256]{1,0:T(8,128)(2,1)S(1)} %bitcast.26, bf16[4096,1792]{1,0:T(8,128)(2,1)} %all-gather.6.cloned.1.call-done), kind=kOutput, calls=%fused_computation.8 | convolution fusion | flops 3758555136 | bytes 17694720 | tf_op jit(solution)/shard_map/dot_general | solution.py:32
  218.6 76.5 %all-gather.8.cloned.1.call-done = bf16[4096,1792]{1,0:T(8,128)(2,1)} async-done(((bf16[256,1792]{1,0:T(8,128)(2,1)}), bf16[4096,1792]{1,0:T(8,128)(2,1)}) %all-gather.8.cloned.1.call-update) | async-done | bytes 14680080 | tf_op jit(solution)/shard_map/all_gather | solution.py:81
  295.1 0.0 copy-start
  295.1 0.0 copy-start.1
  295.1 8.5 %convolution_convert_fusion = bf16[256,1792]{1,0:T(8,128)(2,1)} fusion(bf16[4096,256]{1,0:T(8,128)(2,1)S(1)} %bitcast.27, bf16[4096,1792]{1,0:T(8,128)(2,1)} %all-gather.8.cloned.1.call-done), kind=kOutput, calls=%fused_computation.7 | convolution fusion | flops 3758555136 | bytes 17694720 | tf_op jit(solution)/shard_map/dot_general | solution.py:32
  303.6 1.2 copy-done
  304.8 2.7 fusion.15
  307.4 1.7 copy-done.1
  309.1 2.7 fusion.18
Async XLA Ops:
  7.2 77.3 %copy-start.4 = (bf16[256,1792]{1,0:T(8,128)(2,1)S(1)}, bf16[256,1792]{1,0:T(8,128)(2,1)}, u32[]{:S(2)}) copy-start(bf16[256,1792]{1,0:T(8,128)(2,1)} %param.7) | copy-start | bytes 2752516
  7.2 77.3 %copy-start.3 = (bf16[256,1792]{1,0:T(8,128)(2,1)S(1)}, bf16[256,1792]{1,0:T(8,128)(2,1)}, u32[]{:S(2)}) copy-start(bf16[256,1792]{1,0:T(8,128)(2,1)} %param.6) | copy-start | bytes 2752516
  7.2 77.3 %all-gather.4.cloned.1.call-start = ((), (), s32[]{:S(2)}) async-start(), calls=%async_computation.2 | async-start | bytes 4718592 | tf_op jit(solution)/shard_map/all_gather | solution.py:12
  10.4 199.9 %all-gather.6.cloned.1.call-start = ((), (), s32[]{:S(2)}) async-start(), calls=%async_computation.3 | async-start | bytes 15597568 | tf_op jit(solution)/shard_map/all_gather | solution.py:80
  96.2 198.9 %all-gather.8.cloned.1.call-start = ((), (), s32[]{:S(2)}) async-start(), calls=%async_computation.4 | async-start | bytes 15597568 | tf_op jit(solution)/shard_map/all_gather | solution.py:81
  137.3 53.2 %all-to-all-start = ((bf16[256,16,256]{0,2,1:T(8,128)(2,1)}), bf16[256,16,256]{0,2,1:T(8,128)(2,1)S(1)}, u32[]{:S(2)}, u32[]{:S(2)}) async-start(bf16[256,16,256]{0,2,1:T(8,128)(2,1)} %bitcast), calls=%async_computation | async-start | bytes 4194304 | tf_op jit(solution)/shard_map/all_to_all | solution.py:53
  190.5 1.3 copy-start.2
  295.1 9.7 %copy-start = (bf16[4096,1792]{1,0:T(8,128)(2,1)S(1)}, bf16[4096,1792]{1,0:T(8,128)(2,1)}, u32[]{:S(2)}) copy-start(bf16[4096,1792]{1,0:T(8,128)(2,1)} %all-gather.6.cloned.1.call-done) | copy-start | bytes 44040196
  295.1 14.0 %copy-start.1 = (bf16[4096,1792]{1,0:T(8,128)(2,1)S(1)}, bf16[4096,1792]{1,0:T(8,128)(2,1)}, u32[]{:S(2)}) copy-start(bf16[4096,1792]{1,0:T(8,128)(2,1)} %all-gather.8.cloned.1.call-done) | copy-start | bytes 44040196
Sparse Core Ops, SparseCore 0:
  10.9 73.5 all-gather.3
  96.3 113.8 all-gather.5
  212.5 82.5 all-gather.7
where the time goes:
time: 320 us; the launch traced here: 318 us
  waiting for transfers between devices  214 us (67%)
  matrix products  36.3 us (11%)
  blocking collectives  30.6 us (10%)
  local copies, waits for them, and re-layouts  16.6 us (5%)
  between operations  13.8 us (4%)
  starting transfers between devices  5.65 us (2%)
    all_gather x1, waiting for transfers between devices, on_device(): up_sums = accumulate_one(lax.all_gather(up_grad, 'dp', axis=0, tiled=True))  76.5 us
    all_gather x1, waiting for transfers between devices, sent_together(): whole, at, outs = (lax.all_gather(both, axis, axis=dim, tiled=True), 0, [])  74.1 us
    all_to_all x1, waiting for transfers between devices, on_device(): lax.all_to_all(split, 'dp', split_axis=1, concat_axis=0, tiled=True)  46.8 us
    all_to_all x1, blocking collectives, summed_on_arrival(): lax.all_to_all(tiles, axis, split_axis=0, concat_axis=0, tiled=True)  30.6 us
    dot_general x4, matrix products, inner(): lax.dot_general(left, right, (((0,), (0,)), ((), ())), preferred_element_...  22.1 us
    all_gather x1, waiting for transfers between devices, on_device(): lax.all_gather(gate_grad, 'dp', axis=0, tiled=True)  15.5 us
    dot_general x1, matrix products, on_device(): lax.dot_general(grad_full, down_weight, (((1,), (1,)), ((), ())), preferr...  11.7 us
    unnamed x12, local copies, waits for them, and re-layouts  6.5 us
  transfers between devices with their start and end apart: 4, of which 4 were waited for; matrix products, arithmetic and copies ran while one was open for 7% of the time, Pallas kernels for 0%

commit v1 on v0

v1 whole, which is shorter than its diff:
```python
import jax
import jax.numpy as jnp
from jax import lax
from jax.experimental import pallas as pl
from jax.experimental.pallas import tpu as pltpu
from jax.sharding import PartitionSpec as P

MESH = pl.DeviceIdType.MESH
BF = jnp.bfloat16
F32 = jnp.float32

TOK = 256
NA = 64
NB = TOK - NA
D = 4096
DS = 512
H = 1792
CH = 128
CW = 2 * CH
NC = H // CH
BC = 7
HB = 896
T4 = 4 * TOK
DB = 1024
CR = 112
KSLOTS = 4


def kernel(
    x_hbm, gp_hbm, up_hbm, og_hbm, w_hbm,
    gw_ref, uw_ref, ic_ref, gc_ref, uc_ref,
    og, w, gp, up, g, xin, xt, ks, crv, fin, zs, zr, rt, cv, ccr, zcs, zcr, ic, icr, zis, zir,
    loc, wsem,
    oa_s, oa_r, ob_s, ob_r, xs_s, xs_r, xg_s, xg_r,
    a_s, a_r, af_s, af_r, b_s, b_r, bf_s, bf_r,
    k_s, k_r, z_s, z_r, m_s, m_r,
):
    dp = lax.axis_index("dp")
    t = lax.axis_index("tensor")
    x, zl, c = dp // 4, (dp // 2) % 2, dp % 2
    zh, y = t // 4, t % 4
    xp, xm, x2 = (x + 1) % 4, (x + 3) % 4, (x + 2) % 4
    yp, ym, y2 = (y + 1) % 4, (y + 3) % 4, (y + 2) % 4
    inplane = zl * 2 + c

    def at_x(v):
        return (v * 4 + inplane, t)

    def at_t(zz, yy):
        return (dp, zz * 4 + yy)

    mate = (dp + 1 - 2 * c, t)
    across = (dp + 2 - 4 * zl, t)
    zo = 1 - zh

    def rc(src, dst, ss, rs, dev):
        return pltpu.make_async_remote_copy(
            src_ref=src, dst_ref=dst, send_sem=ss, recv_sem=rs, device_id=dev, device_id_type=MESH
        )

    l_gp = pltpu.make_async_copy(gp_hbm, gp, loc.at[0])
    l_up = pltpu.make_async_copy(up_hbm, up, loc.at[1])
    own_cols = pl.ds(pl.multiple_of(t * DS, DS), DS)
    l_og = pltpu.make_async_copy(og_hbm, og.at[:, own_cols], loc.at[2])
    l_og.start()
    l_gp.start()
    l_up.start()

    def w_copy(j):
        r = pl.ds(pl.multiple_of(j * CH, CH), CH)
        return pltpu.make_async_copy(w_hbm.at[r, :], w.at[r, :], wsem.at[j])

    @pl.loop(0, NC)
    def _(j):
        w_copy(j).start()

    barrier = pltpu.get_barrier_semaphore()

    def here(dev):
        pl.semaphore_signal(barrier, inc=1, device_id=dev, device_id_type=MESH)

    for dz in range(2):
        for dy in range(4):
            if (dz, dy) != (0, 0):
                here(at_t((zh + dz) % 2, (y + dy) % 4))
    here(at_x(xp))
    here(at_x(xm))
    here(mate)
    here(across)
    xd = 2 * zh + y // 2
    half = y % 2
    self_x = xd == x
    for k in range(8):
        sx, sy, sz = k // 2, 2 * (x % 2) + k % 2, x // 2
        mine = jnp.logical_and(sx == x, jnp.logical_and(sy == y, sz == zh))

        @pl.when(jnp.logical_not(mine))
        def _():
            here((sx * 4 + inplane, sz * 4 + sy))

    pl.semaphore_wait(barrier, 19 - jnp.where(self_x, 1, 0))

    oa = []
    for dz in range(2):
        for dy in range(4):
            if (dz, dy) != (0, 0):
                cp = rc(
                    og_hbm.at[pl.ds(0, NA), :],
                    og.at[pl.ds(0, NA), own_cols],
                    oa_s.at[dz, dy],
                    oa_r.at[dz, dy],
                    at_t((zh + dz) % 2, (y + dy) % 4),
                )
                cp.start()
                oa.append(cp)

    half_cols = pl.ds(pl.multiple_of(half * DS, DS), DS)

    def scatter(k):
        return rc(
            x_hbm.at[pl.ds(k * 32, 32), :],
            xin.at[x, k, :, half_cols],
            xs_s.at[k],
            xs_r.at[x * 2 + half],
            (xd * 4 + inplane, k),
        )

    own_piece = pltpu.make_async_copy(
        x_hbm.at[pl.ds(pl.multiple_of(t * 32, 32), 32), :],
        xin.at[x, t, :, half_cols],
        xs_r.at[x * 2 + half],
    )
    for k in range(8):
        is_me = jnp.logical_and(self_x, t == k)

        @pl.when(is_me)
        def _():
            own_piece.start()

        @pl.when(jnp.logical_not(is_me))
        def _():
            scatter(k).start()

    def og_part(owner, part):
        cols = pl.ds(pl.multiple_of(owner * DS, DS), DS)
        rows = {0: pl.ds(NA, NB), 1: pl.ds(NA, NB // 2), 2: pl.ds(NA + NB // 2, NB // 2)}[part]
        return og.at[rows, cols]

    def x_part(owner, part):
        lead = {0: pl.ds(0, 4), 1: pl.ds(0, 2), 2: pl.ds(2, 2)}[part]
        return xin.at[lead, owner]

    def gather(part_of, first, ss, rs):
        def step(i):
            if i < 3:
                dev = (at_t(zo, y), at_t(zh, yp), at_t(zh, ym))[i]
                return rc(first, part_of(t, 0), ss.at[i], rs.at[i], dev)
            if i < 5:
                dev = (at_t(zh, yp), at_t(zh, ym))[i - 3]
                blk = part_of(zo * 4 + y, 0)
                return rc(blk, blk, ss.at[i], rs.at[i], dev)
            zz = (zh, zo)[(i - 5) // 2]
            if i % 2 == 1:
                blk = part_of(zz * 4 + ym, 1)
                return rc(blk, blk, ss.at[i], rs.at[i], at_t(zh, yp))
            blk = part_of(zz * 4 + yp, 2)
            return rc(blk, blk, ss.at[i], rs.at[i], at_t(zh, ym))

        def landed(i):
            where = (
                part_of(zo * 4 + y, 0), part_of(zh * 4 + ym, 0), part_of(zh * 4 + yp, 0),
                part_of(zo * 4 + ym, 0), part_of(zo * 4 + yp, 0),
                part_of(zh * 4 + y2, 1), part_of(zh * 4 + y2, 2),
                part_of(zo * 4 + y2, 1), part_of(zo * 4 + y2, 2),
            )[i]
            rc(where, where, ss.at[i], rs.at[i], at_t(zo, y)).wait_recv()

        return step, landed

    ob_step, ob_landed = gather(og_part, og_hbm.at[pl.ds(NA, NB), :], ob_s, ob_r)
    xg_step, xg_landed = gather(x_part, x_part(t, 0), xg_s, xg_r)
    for i in range(3):
        ob_step(i).start()

    for k in range(8):
        sx, sh = k // 2, k % 2
        dst = xin.at[sx, t, :, pl.ds(sh * DS, DS)]
        rc(dst, dst, xs_s.at[0], xs_r.at[k], mate).wait_recv()
    for i in range(3):
        xg_step(i).start()

    l_og.wait()
    l_gp.wait()
    l_up.wait()
    for dz in range(2):
        for dy in range(4):
            if (dz, dy) != (0, 0):
                oc = ((zh + 2 - dz) % 2) * 4 + (y + 4 - dy) % 4
                dst = og.at[pl.ds(0, NA), pl.ds(pl.multiple_of(oc * DS, DS), DS)]
                rc(dst, dst, oa_s.at[dz, dy], oa_r.at[dz, dy], mate).wait_recv()

    def grads(j, r0, n):
        hid = pl.ds(pl.multiple_of(j * CH, CH), CH)
        hg = lax.dot_general(
            og[pl.ds(r0, n), :], w[hid, :], (((1,), (1,)), ((), ())), preferred_element_type=F32
        )
        gate = gp[pl.ds(r0, n), hid].astype(F32)
        upv = up[pl.ds(r0, n), hid].astype(F32)
        sig = jax.nn.sigmoid(gate)
        hs = hg * sig
        rows = pl.ds(pl.multiple_of(x * TOK + r0, 16), n)
        g[j, rows, pl.ds(0, CH)] = (hs * upv * (1.0 + gate * (1.0 - sig))).astype(BF)
        g[j, rows, pl.ds(CH, CH)] = (hs * gate).astype(BF)

    def xrows(xx, r0, n):
        return pl.ds(pl.multiple_of(xx * TOK + r0, 16), n)

    def ring(r0, n, s_s, s_r, f_s, f_r):
        h = n // 2

        def send(j, way):
            blk = g.at[j, xrows(x, r0, n), :]
            return rc(blk, blk, s_s.at[j, way], s_r.at[j, way], at_x((xp, xm)[way]))

        def landed(j, way):
            blk = g.at[j, xrows((xm, xp)[way], r0, n), :]
            rc(blk, blk, s_s.at[j, way], s_r.at[j, way], at_x(xp)).wait_recv()

        def forward(j, way):
            blk = g.at[j, xrows((xm, xp)[way], r0 + way * h, h), :]
            return rc(blk, blk, f_s.at[j, way], f_r.at[j, way], at_x((xp, xm)[way]))

        def far_landed(j, way):
            blk = g.at[j, xrows(x2, r0 + way * h, h), :]
            rc(blk, blk, f_s.at[j, way], f_r.at[j, way], at_x(xp)).wait_recv()

        def pass_on(j):
            for way in range(2):
                landed(j, way)
                forward(j, way).start()

        return send, pass_on, forward, far_landed

    a_send, a_pass, a_fwd, a_far = ring(0, NA, a_s, a_r, af_s, af_r)
    b_send, b_pass, b_fwd, b_far = ring(NA, NB, b_s, b_r, bf_s, bf_r)

    @pl.loop(0, NC)
    def _(j):
        w_copy(j).wait()
        grads(j, 0, NA)
        a_send(j, 0).start()
        a_send(j, 1).start()

        @pl.when(j >= 2)
        def _():
            a_pass(j - 2)

        @pl.when(j == 2)
        def _():
            ob_landed(0)
            ob_step(3).start()
            ob_step(4).start()

        @pl.when(j == 4)
        def _():
            ob_landed(1)
            ob_landed(2)
            ob_step(5).start()
            ob_step(6).start()

        @pl.when(j == 5)
        def _():
            xg_landed(0)
            xg_step(3).start()
            xg_step(4).start()

        @pl.when(j == 7)
        def _():
            ob_landed(3)
            ob_landed(4)
            ob_step(7).start()
            ob_step(8).start()

        @pl.when(j == 9)
        def _():
            xg_landed(1)
            xg_landed(2)
            xg_step(5).start()
            xg_step(6).start()

    a_pass(NC - 2)
    a_pass(NC - 1)
    for i in range(5, 9):
        ob_landed(i)

    slots = ((1 - zl) * 2 + 1 - c, zl * 2 + 1 - c, (1 - zl) * 2 + c, zl * 2 + c)

    def build_xt():
        for i in range(5, 9):
            xg_landed(i)
        for s in range(4):
            cols = pl.ds(pl.multiple_of(slots[s] * 256, 256), 256)
            blk = xin[:, :, :, cols].reshape(T4, 256)
            xt[pl.ds(s * 256, 256), :] = blk.T
        for s in range(4):
            rows = xt[pl.ds(pl.multiple_of(s * 256 + t * 32, 32), 32), :]
            ic[pl.ds(s * 32, 32), :] = jnp.dot(
                rows, xin[...].reshape(T4, DB), preferred_element_type=F32
            )
        rc(ic.at[pl.ds(0, 64), :], icr, m_s.at[0], m_r.at[0], mate).start()

    def k_copy(j):
        return rc(
            ks.at[j % KSLOTS, pl.ds(0, 512), :], crv.at[j % KSLOTS], k_s.at[j], k_r.at[j], mate
        )

    def z_copy(j):
        return rc(zs.at[j], zr.at[j], z_s.at[j], z_r.at[j], across)

    def cov_copy(zz):
        rows = pl.ds(pl.multiple_of(64 * (x % 2) + (zz * 2 + 1 - c) * CR, 16), CR)
        return rc(cv.at[:, rows, :], ccr.at[zz], m_s.at[2 + zz], m_r.at[2 + zz], mate)

    zcov_copy = rc(zcs, zcr, m_s.at[4], m_r.at[4], across)

    def own_cov(zz, a):
        rows = pl.ds(pl.multiple_of(64 * (x % 2) + (zz * 2 + c) * CR, 16), CR)
        return cv[a, rows, :] + ccr[zz, a]

    def cov():
        b = x // 2
        for k in range(4):
            blk = g[BC * b + 3 * (x % 2) + k].T
            rt[0, pl.ds(k * CH, CH), :] = blk[:CH]
            rt[1, pl.ds(k * CH, CH), :] = blk[CH:]

        @pl.loop(0, BC)
        def _(k):
            cols = pl.ds(pl.multiple_of(k * CH, CH), CH)
            for a in range(2):
                cv[a, :, cols] = jnp.dot(
                    rt[a], g[BC * b + k, :, pl.ds(a * CH, CH)], preferred_element_type=F32
                )

        cov_copy(0).start()
        cov_copy(1).start()

    def cov_across():
        cov_copy(0).wait_recv()
        cov_copy(1).wait_recv()
        for a in range(2):
            zcs[a] = own_cov(1 - zl, a).astype(BF)
        zcov_copy.start()

    in_across = rc(zis, zir, m_s.at[1], m_r.at[1], across)

    @pl.loop(0, NC + 4)
    def _(j):
        @pl.when(j < NC)
        def _():
            grads(j, NA, NB)
            b_send(j, 0).start()
            b_send(j, 1).start()

        @pl.when(j == 0)
        def _():
            xg_landed(3)
            xg_landed(4)
            xg_step(7).start()
            xg_step(8).start()

        @pl.when(jnp.logical_and(j >= 1, j < NC + 1))
        def _():
            b_pass(j - 1)

        @pl.when(j == 2)
        def _():
            build_xt()

        @pl.when(jnp.logical_and(j >= 2, j < NC + 2))
        def _():
            i = j - 2
            for way in range(2):
                a_far(i, way)
                b_far(i, way)

            @pl.when(i >= KSLOTS)
            def _():
                k_copy(i - KSLOTS).wait_send()

            for m in range(4):
                ks[i % KSLOTS, pl.ds(m * 256, 256), :] = jnp.dot(
                    xt[pl.ds(m * 256, 256), :], g[i], preferred_element_type=F32
                )
            k_copy(i).start()

        @pl.when(jnp.logical_and(j >= 3, j < NC + 3))
        def _():
            i = j - 3
            k_copy(i).wait_recv()
            s = i % KSLOTS
            zs[i] = (ks[s, pl.ds(512, 256), :] + crv[s, pl.ds(0, 256), :]).astype(BF)
            z_copy(i).start()
            fin[i] = ks[s, pl.ds(768, 256), :] + crv[s, pl.ds(256, 256), :]

        @pl.when(j == 5)
        def _():
            rc(ic.at[pl.ds(0, 64), :], icr, m_s.at[0], m_r.at[0], mate).wait_recv()
            zis[...] = ic[pl.ds(64, 32), :] + icr[pl.ds(0, 32), :]
            in_across.start()

        @pl.when(jnp.logical_and(j == BC + 1, x < 2))
        def _():
            cov()

        @pl.when(jnp.logical_and(j == BC + 2, x < 2))
        def _():
            cov_across()

        @pl.when(jnp.logical_and(j == NC + 1, x >= 2))
        def _():
            cov()

        @pl.when(jnp.logical_and(j == NC + 2, x >= 2))
        def _():
            cov_across()

        @pl.when(j >= 4)
        def _():
            i = j - 4
            z_copy(i).wait_recv()
            tot = fin[i] + zr[i].astype(F32)
            hid = pl.ds(pl.multiple_of(i * CH, CH), CH)
            gw_ref[:, hid] = tot[:, :CH].astype(BF)
            uw_ref[:, hid] = tot[:, CH:].astype(BF)

    in_across.wait_recv()
    ic_ref[...] = (
        ic[pl.ds(96, 32), :] + icr[pl.ds(32, 32), :] + zir[...]
    ) * (1.0 / 4096.0)
    zcov_copy.wait_recv()
    gc_ref[...] = own_cov(zl, 0) + zcr[0].astype(F32)
    uc_ref[...] = own_cov(zl, 1) + zcr[1].astype(F32)

    for cp in oa:
        cp.wait_send()
    for i in range(9):
        ob_step(i).wait_send()
        xg_step(i).wait_send()
    for k in range(8):

        @pl.when(jnp.logical_not(jnp.logical_and(self_x, t == k)))
        def _():
            scatter(k).wait_send()

    @pl.loop(0, NC)
    def _(j):
        for way in range(2):
            a_send(j, way).wait_send()
            a_fwd(j, way).wait_send()
            b_send(j, way).wait_send()
            b_fwd(j, way).wait_send()
        z_copy(j).wait_send()

        @pl.when(j >= NC - KSLOTS)
        def _():
            k_copy(j).wait_send()

    rc(ic.at[pl.ds(0, 64), :], icr, m_s.at[0], m_r.at[0], mate).wait_send()
    in_across.wait_send()
    cov_copy(0).wait_send()
    cov_copy(1).wait_send()
    zcov_copy.wait_send()


def on_device(inputs, gate_pre, up_pre, out_grad, down_weight):
    dma = pltpu.SemaphoreType.DMA
    vm = pltpu.VMEM
    outs = pl.pallas_call(
        kernel,
        out_shape=(
            jax.ShapeDtypeStruct((TOK, H), BF),
            jax.ShapeDtypeStruct((TOK, H), BF),
            jax.ShapeDtypeStruct((32, DB), F32),
            jax.ShapeDtypeStruct((CR, HB), F32),
            jax.ShapeDtypeStruct((CR, HB), F32),
        ),
        in_specs=[pl.BlockSpec(memory_space=pl.ANY)] * 5,
        out_specs=tuple([pl.BlockSpec(memory_space=vm)] * 5),
        scratch_shapes=[
            vm((TOK, D), BF),
            vm((H, D), BF),
            vm((TOK, H), BF),
            vm((TOK, H), BF),
            vm((NC, T4, CW), BF),
            vm((4, 8, 32, DB), BF),
            vm((DB, T4), BF),
            vm((KSLOTS, DB, CW), F32),
            vm((KSLOTS, 512, CW), F32),
            vm((NC, TOK, CW), F32),
            vm((NC, TOK, CW), BF),
            vm((NC, TOK, CW), BF),
            vm((2, 512, T4), BF),
            vm((2, 512, HB), F32),
            vm((2, 2, CR, HB), F32),
            vm((2, CR, HB), BF),
            vm((2, CR, HB), BF),
            vm((128, DB), F32),
            vm((64, DB), F32),
            vm((32, DB), F32),
            vm((32, DB), F32),
            dma((3,)),
            dma((NC,)),
            dma((2, 4)), dma((2, 4)),
            dma((9,)), dma((9,)),
            dma((8,)), dma((8,)),
            dma((9,)), dma((9,)),
            dma((NC, 2)), dma((NC, 2)), dma((NC, 2)), dma((NC, 2)),
            dma((NC, 2)), dma((NC, 2)), dma((NC, 2)), dma((NC, 2)),
            dma((NC,)), dma((NC,)),
            dma((NC,)), dma((NC,)),
            dma((5,)), dma((5,)),
        ],
        compiler_params=pltpu.CompilerParams(
            collective_id=0, has_side_effects=True, vmem_limit_bytes=62 << 20
        ),
    )(inputs, gate_pre, up_pre, out_grad, down_weight)
    gw, uw, ic, gc, uc = outs
    return gw, uw, ic, gc[None], uc[None]


def solution(mesh):
    placed = (
        P("dp", "tensor"),
        P("dp", "tensor"),
        P("dp", "tensor"),
        P("dp", "tensor"),
        P("tensor", None),
    )
    return jax.shard_map(
        on_device,
        mesh=mesh,
        in_specs=placed,
        out_specs=(
            P("dp", "tensor"),
            P("dp", "tensor"),
            P(("dp", "tensor"), None),
            P("tensor", "dp", None),
            P("tensor", "dp", None),
        ),
        check_vma=False,
    )
```

time: 320 us -> 152 us (0.47)
  waiting for transfers between devices: 214 us -> 0 us
  Pallas kernels: 0 us -> 142 us
  matrix products: 36.3 us -> 0 us
  blocking collectives: 30.6 us -> 0 us
  between operations: 13.8 us -> 0.64 us
  local copies, waits for them, and re-layouts: 16.6 us -> 9.43 us
  starting transfers between devices: 5.65 us -> 0 us
    all_gather x3 -> x0, waiting for transfers between devices: 166 us -> none  [the longest x1 76.5 us: on_device(): up_sums = accumulate_one(lax.all_gather(up_grad, 'dp', axis=0, tiled=True))]
    pallas_call x0 -> x1, Pallas kernels: none -> 142 us  [on_device(): pl.pallas_call(kernel, out_shape=(jax.ShapeDtypeStruct((TOK, H), BF), jax...]
    all_to_all x1 -> x0, waiting for transfers between devices: 46.8 us -> none  [on_device(): lax.all_to_all(split, 'dp', split_axis=1, concat_axis=0, tiled=True)]
    dot_general x6 -> x0, matrix products: 36.3 us -> none  [the longest x4 22.1 us: inner(): lax.dot_general(left, right, (((0,), (0,)), ((), ())), preferred_element_...]
    all_to_all x1 -> x0, blocking collectives: 30.6 us -> none  [summed_on_arrival(): lax.all_to_all(tiles, axis, split_axis=0, concat_axis=0, tiled=True)]
    all_to_all x1 -> x0, starting transfers between devices: 5.53 us -> none  [on_device(): lax.all_to_all(split, 'dp', split_axis=1, concat_axis=0, tiled=True)]
    unnamed x12 -> x5, local copies, waits for them, and re-layouts: 6.5 us -> 9.43 us
  transfers between devices with their start and end apart: 4 -> 0, of which waited for: 4 -> 0; matrix products, arithmetic and copies ran while one was open for 7% -> 0% of each run, Pallas kernels for 0% -> 0%
where the time goes in v1:
time: 152 us
  Pallas kernels  142 us (93%)
  local copies, waits for them, and re-layouts  9.43 us (6%)
    pallas_call x1, Pallas kernels, on_device(): pl.pallas_call(kernel, out_shape=(jax.ShapeDtypeStruct((TOK, H), BF), jax...  142 us
    unnamed x5, local copies, waits for them, and re-layouts  9.43 us

profile of v1, /device:TPU:7, one launch (start us, length us, event | category | flops | bytes accessed | tf_op | source)
XLA Modules:
  0.0 151.9 jit_solution(13537867528947489030)
XLA Ops:
  0.6 141.8 %shard_map.92 = (bf16[256,1792]{1,0:T(8,128)(2,1)}, bf16[256,1792]{1,0:T(8,128)(2,1)}, f32[32,1024]{1,0:T(8,128)}, f32[112,896]{1,0:T(8,128)}, f32[112,896]{1,0:T(8,128)}) custom-call(bf16[256,512]{1,0:T(8,128)(2,1)} %x_hbm.1, bf16[256,1792]{1,0:T(8,128)(2,1)} %gp_hbm.1, bf16[256,1792]{1,0:T(8,128)(2,1)} %up_hbm.1, bf16[256,512]{1,0:T(8,128)(2,1)} %og_hbm.1, ...), custom_call_target="tpu_custom_call" | custom-call | tf_op jit(solution)/shard_map/pallas_call | solution.py:479
  142.5 2.2 %copy.15 = bf16[256,1792]{1,0:T(8,128)(2,1)} copy(bf16[256,1792]{1,0:T(8,128)(2,1)} %get-tuple-element.20) | data formatting | bytes 1835008
  144.6 2.2 %copy.16 = bf16[256,1792]{1,0:T(8,128)(2,1)} copy(bf16[256,1792]{1,0:T(8,128)(2,1)} %get-tuple-element.21) | data formatting | bytes 1835008
  146.8 1.6 %copy.17 = f32[32,1024]{1,0:T(8,128)} copy(f32[32,1024]{1,0:T(8,128)} %get-tuple-element.22) | data formatting | bytes 262144
  148.4 1.8 %copy.18 = f32[1,112,896]{2,1,0:T(8,128)} copy(f32[1,112,896]{2,1,0:T(8,128)} %bitcast.3) | data formatting | bytes 802816
  150.1 1.8 %copy.19 = f32[1,112,896]{2,1,0:T(8,128)} copy(f32[1,112,896]{2,1,0:T(8,128)} %bitcast.2) | data formatting | bytes 802816

commit v2 on v1

v2 whole, which is shorter than its diff:
```python
import jax
import jax.numpy as jnp
from jax import lax
from jax.experimental import pallas as pl
from jax.experimental.pallas import tpu as pltpu
from jax.sharding import PartitionSpec as P

MESH = pl.DeviceIdType.MESH
BF = jnp.bfloat16
F32 = jnp.float32

TOK = 256
NA = 64
NB = TOK - NA
D = 4096
DS = 512
H = 1792
CH = 128
CW = 2 * CH
NC = H // CH
BC = 7
HB = 896
T4 = 4 * TOK
DB = 1024
CR = 112
KSLOTS = 4
X0 = 4
ZLAG = 9


def kernel(
    x_hbm, gp_hbm, up_hbm, og_hbm, w_hbm,
    gw_hbm, uw_hbm, ic_hbm, gc_hbm, uc_hbm,
    og, w, gp, up, g, xs, xin, xt, ks, crv, fin, zs, zr, rt, cv, ccr, zcs, zcr, ic, icr, zis, zir, out,
    loc, wsem, osem,
    oa_s, oa_r, ob_s, ob_r, xs_s, xs_r, x2_s, x2_r, xg_s, xg_r,
    a_s, a_r, af_s, af_r, b_s, b_r, bf_s, bf_r,
    k_s, k_r, z_s, z_r, m_s, m_r,
):
    dp = lax.axis_index("dp")
    t = lax.axis_index("tensor")
    x, zl, c = dp // 4, (dp // 2) % 2, dp % 2
    zh, y = t // 4, t % 4
    xp, xm, x2 = (x + 1) % 4, (x + 3) % 4, (x + 2) % 4
    yp, ym, y2 = (y + 1) % 4, (y + 3) % 4, (y + 2) % 4
    inplane = zl * 2 + c

    def at_x(v):
        return (v * 4 + inplane, t)

    def at_t(zz, yy):
        return (dp, zz * 4 + yy)

    mate = (dp + 1 - 2 * c, t)
    across = (dp + 2 - 4 * zl, t)
    zo = 1 - zh
    peers = [(dz, dy) for dz in range(2) for dy in range(4) if (dz, dy) != (0, 0)]

    def to_peer(dz, dy):
        return (zh + dz) % 2, (y + dy) % 4

    def from_peer(dz, dy):
        return ((zh + 2 - dz) % 2) * 4 + (y + 4 - dy) % 4

    def rc(src, dst, ss, rs, dev):
        return pltpu.make_async_remote_copy(
            src_ref=src, dst_ref=dst, send_sem=ss, recv_sem=rs, device_id=dev, device_id_type=MESH
        )

    l_gp = pltpu.make_async_copy(gp_hbm, gp, loc.at[0])
    l_up = pltpu.make_async_copy(up_hbm, up, loc.at[1])
    own_cols = pl.ds(pl.multiple_of(t * DS, DS), DS)
    l_og = pltpu.make_async_copy(og_hbm, og.at[:, own_cols], loc.at[2])
    l_xs = pltpu.make_async_copy(
        x_hbm.at[pl.ds(pl.multiple_of(t * 32, 32), 32), :], xs.at[t], loc.at[3]
    )
    l_og.start()
    l_xs.start()
    l_gp.start()
    l_up.start()

    def w_copy(j):
        r = pl.ds(pl.multiple_of(j * CH, CH), CH)
        return pltpu.make_async_copy(w_hbm.at[r, :], w.at[r, :], wsem.at[j])

    @pl.loop(0, NC)
    def _(j):
        w_copy(j).start()

    barrier = pltpu.get_barrier_semaphore()
    greeted = [at_t(*to_peer(dz, dy)) for dz, dy in peers]
    greeted += [at_x(xp), at_x(xm), at_x(x2), mate, across]
    for dev in greeted:
        pl.semaphore_signal(barrier, inc=1, device_id=dev, device_id_type=MESH)
    pl.semaphore_wait(barrier, len(greeted))

    def oa_copy(dz, dy):
        return rc(
            og_hbm.at[pl.ds(0, NA), :],
            og.at[pl.ds(0, NA), own_cols],
            oa_s.at[dz, dy],
            oa_r.at[dz, dy],
            at_t(*to_peer(dz, dy)),
        )

    for dz, dy in peers:
        oa_copy(dz, dy).start()

    def spread(dz, dy):
        zz, yy = to_peer(dz, dy)
        rows = pl.ds(pl.multiple_of((zz * 4 + yy) * 32, 32), 32)
        return rc(
            x_hbm.at[rows, :], xs.at[t], xs_s.at[dz, dy], xs_r.at[dz, dy], at_t(zz, yy)
        )

    for dz, dy in peers:
        spread(dz, dy).start()

    def to_x(dx):
        v = (x + dx) % 4
        return rc(
            xs.at[pl.ds(2 * v, 2)], xin.at[:, x, t], x2_s.at[dx - 1], x2_r.at[dx - 1], at_x(v)
        )

    def all_to_x():
        l_xs.wait()
        for dz, dy in peers:
            dst = xs.at[from_peer(dz, dy)]
            rc(dst, dst, xs_s.at[dz, dy], xs_r.at[dz, dy], mate).wait_recv()
        for dx in (2, 1, 3):
            to_x(dx).start()
        pltpu.make_async_copy(xs.at[pl.ds(2 * x, 2)], xin.at[:, x, t], loc.at[4]).start()

    def from_x():
        pltpu.make_async_copy(xs.at[pl.ds(2 * x, 2)], xin.at[:, x, t], loc.at[4]).wait()
        for dx in (1, 2, 3):
            dst = xin.at[:, (x + 4 - dx) % 4, t]
            rc(dst, dst, x2_s.at[dx - 1], x2_r.at[dx - 1], mate).wait_recv()

    def og_part(owner, part):
        cols = pl.ds(pl.multiple_of(owner * DS, DS), DS)
        at, n = ((0, NB), (0, NB // 2), (NB // 2, NB // 2), (0, NB // 4), (NB // 4, NB // 4))[part]
        return og.at[pl.ds(NA + at, n), cols]

    def x_part(owner, part):
        at, n = ((0, 4), (0, 2), (2, 2), (0, 1), (1, 1))[part]
        return xin.at[:, pl.ds(at, n), owner]

    def gather(part_of, first, ss, rs):
        up1, dn1, zp = at_t(zh, yp), at_t(zh, ym), at_t(zo, y)
        out = (
            (t, 0, zp), (t, 0, up1), (t, 0, dn1),
            (zo * 4 + y, 1, up1), (zo * 4 + y, 1, dn1),
            (zh * 4 + ym, 1, up1), (zh * 4 + yp, 2, dn1),
            (zo * 4 + ym, 3, up1), (zo * 4 + yp, 4, dn1),
            (zh * 4 + ym, 2, zp), (zh * 4 + yp, 2, zp), (zh * 4 + y2, 2, zp),
        )
        come = (
            (zo * 4 + y, 0), (zh * 4 + ym, 0), (zh * 4 + yp, 0),
            (zo * 4 + ym, 1), (zo * 4 + yp, 1),
            (zh * 4 + y2, 1), (zh * 4 + y2, 2),
            (zo * 4 + y2, 3), (zo * 4 + y2, 4),
            (zo * 4 + ym, 2), (zo * 4 + yp, 2), (zo * 4 + y2, 2),
        )

        def step(i):
            owner, part, dev = out[i]
            dst = part_of(owner, part)
            return rc(first if i < 3 else dst, dst, ss.at[i], rs.at[i], dev)

        def landed(*which):
            for i in which:
                dst = part_of(*come[i])
                rc(dst, dst, ss.at[i], rs.at[i], zp).wait_recv()

        def go(*which):
            for i in which:
                step(i).start()

        return step, landed, go

    ob_step, ob_landed, ob_go = gather(og_part, og_hbm.at[pl.ds(NA, NB), :], ob_s, ob_r)
    xg_step, xg_landed, xg_go = gather(x_part, x_part(t, 0), xg_s, xg_r)
    ob_go(0, 1, 2)

    l_og.wait()
    l_gp.wait()
    l_up.wait()
    for dz, dy in peers:
        dst = og.at[pl.ds(0, NA), pl.ds(pl.multiple_of(from_peer(dz, dy) * DS, DS), DS)]
        rc(dst, dst, oa_s.at[dz, dy], oa_r.at[dz, dy], mate).wait_recv()

    def grads(j, r0, n):
        hid = pl.ds(pl.multiple_of(j * CH, CH), CH)
        hg = lax.dot_general(
            og[pl.ds(r0, n), :], w[hid, :], (((1,), (1,)), ((), ())), preferred_element_type=F32
        )
        gate = gp[pl.ds(r0, n), hid].astype(F32)
        upv = up[pl.ds(r0, n), hid].astype(F32)
        sig = jax.nn.sigmoid(gate)
        hs = hg * sig
        rows = pl.ds(pl.multiple_of(x * TOK + r0, 16), n)
        g[j, rows, pl.ds(0, CH)] = (hs * upv * (1.0 + gate * (1.0 - sig))).astype(BF)
        g[j, rows, pl.ds(CH, CH)] = (hs * gate).astype(BF)

    def xrows(xx, r0, n):
        return pl.ds(pl.multiple_of(xx * TOK + r0, 16), n)

    def ring(r0, n, s_s, s_r, f_s, f_r):
        h = n // 2

        def send(j, way):
            blk = g.at[j, xrows(x, r0, n), :]
            return rc(blk, blk, s_s.at[j, way], s_r.at[j, way], at_x((xp, xm)[way]))

        def landed(j, way):
            blk = g.at[j, xrows((xm, xp)[way], r0, n), :]
            rc(blk, blk, s_s.at[j, way], s_r.at[j, way], at_x(xp)).wait_recv()

        def forward(j, way):
            blk = g.at[j, xrows((xm, xp)[way], r0 + way * h, h), :]
            return rc(blk, blk, f_s.at[j, way], f_r.at[j, way], at_x((xp, xm)[way]))

        def far_landed(j, way):
            blk = g.at[j, xrows(x2, r0 + way * h, h), :]
            rc(blk, blk, f_s.at[j, way], f_r.at[j, way], at_x(xp)).wait_recv()

        def pass_on(j):
            for way in range(2):
                landed(j, way)
                forward(j, way).start()

        return send, pass_on, forward, far_landed

    a_send, a_pass, a_fwd, a_far = ring(0, NA, a_s, a_r, af_s, af_r)
    b_send, b_pass, b_fwd, b_far = ring(NA, NB, b_s, b_r, bf_s, bf_r)

    @pl.loop(0, NC)
    def _(j):
        w_copy(j).wait()
        grads(j, 0, NA)
        a_send(j, 0).start()
        a_send(j, 1).start()

        @pl.when(j >= 2)
        def _():
            a_pass(j - 2)

        @pl.when(j == 1)
        def _():
            all_to_x()

        @pl.when(j == 3)
        def _():
            ob_landed(0)
            ob_go(3, 4)

        @pl.when(j == 4)
        def _():
            ob_landed(1, 2)
            ob_go(5, 6, 9, 10)

        @pl.when(j == 6)
        def _():
            from_x()
            xg_go(0, 1, 2)

        @pl.when(j == 8)
        def _():
            ob_landed(3, 4)
            ob_go(7, 8)

        @pl.when(j == 9)
        def _():
            ob_landed(6)
            ob_go(11)

        @pl.when(j == 12)
        def _():
            xg_landed(0)
            xg_go(3, 4)

    a_pass(NC - 2)
    a_pass(NC - 1)
    ob_landed(5, 7, 8, 9, 10, 11)

    slots = ((1 - zl, 1 - c), (zl, 1 - c), (1 - zl, c), (zl, c))
    ic_copy = rc(ic.at[pl.ds(0, 64), :], icr, m_s.at[0], m_r.at[0], mate)
    in_across = rc(zis, zir, m_s.at[1], m_r.at[1], across)

    def build_xt():
        xg_landed(5, 7, 8, 9, 10, 11)
        for s in range(4):
            hi, lo = slots[s]
            cols = pl.ds(pl.multiple_of(lo * 256, 256), 256)
            xt[pl.ds(s * 256, 256), :] = xin[hi, :, :, :, cols].reshape(T4, 256).T

    def in_cov():
        rows = jnp.concatenate(
            [xt[pl.ds(pl.multiple_of(s * 256 + t * 32, 32), 32), :] for s in range(4)], axis=0
        )
        for h in range(2):
            ic[:, pl.ds(h * 512, 512)] = jnp.dot(
                rows, xin[h].reshape(T4, 512), preferred_element_type=F32
            )
        ic_copy.start()

    def k_copy(j):
        return rc(
            ks.at[j % KSLOTS, pl.ds(0, 512), :], crv.at[j % KSLOTS], k_s.at[j], k_r.at[j], mate
        )

    def z_copy(j):
        return rc(zs.at[j], zr.at[j], z_s.at[j], z_r.at[j], across)

    def cov_copy(zz):
        rows = pl.ds(pl.multiple_of(64 * (x % 2) + (zz * 2 + 1 - c) * CR, 16), CR)
        return rc(cv.at[:, rows, :], ccr.at[zz], m_s.at[2 + zz], m_r.at[2 + zz], mate)

    zcov_copy = rc(zcs, zcr, m_s.at[4], m_r.at[4], across)

    def own_cov(zz, a):
        rows = pl.ds(pl.multiple_of(64 * (x % 2) + (zz * 2 + c) * CR, 16), CR)
        return cv[a, rows, :] + ccr[zz, a]

    def cov():
        b = x // 2
        for k in range(4):
            blk = g[BC * b + 3 * (x % 2) + k].T
            rt[0, pl.ds(k * CH, CH), :] = blk[:CH]
            rt[1, pl.ds(k * CH, CH), :] = blk[CH:]

        for a in range(2):
            half = pl.ds(a * CH, CH)

            @pl.loop(0, 3)
            def _(k):
                two = jnp.concatenate(
                    [g[BC * b + 2 * k, :, half], g[BC * b + 2 * k + 1, :, half]], axis=1
                )
                cv[a, :, pl.ds(pl.multiple_of(k * CW, CW), CW)] = jnp.dot(
                    rt[a], two, preferred_element_type=F32
                )

            cv[a, :, pl.ds(6 * CH, CH)] = jnp.dot(
                rt[a], g[BC * b + 6, :, half], preferred_element_type=F32
            )
        cov_copy(0).start()
        cov_copy(1).start()

    def cov_across():
        cov_copy(0).wait_recv()
        cov_copy(1).wait_recv()
        for a in range(2):
            zcs[a] = own_cov(1 - zl, a).astype(BF)
        zcov_copy.start()

    def weigh(i):
        for way in range(2):
            a_far(i, way)
            b_far(i, way)

        @pl.when(i >= KSLOTS)
        def _():
            k_copy(i - KSLOTS).wait_send()

        for m in range(4):
            ks[i % KSLOTS, pl.ds(m * 256, 256), :] = jnp.dot(
                xt[pl.ds(m * 256, 256), :], g[i], preferred_element_type=F32
            )
        k_copy(i).start()

    def combine(i):
        k_copy(i).wait_recv()
        s = i % KSLOTS
        zs[i] = (ks[s, pl.ds(512, 256), :] + crv[s, pl.ds(0, 256), :]).astype(BF)
        z_copy(i).start()
        fin[i] = ks[s, pl.ds(768, 256), :] + crv[s, pl.ds(256, 256), :]

    def out_copy(i, a):
        hid = pl.ds(pl.multiple_of(i * CH, CH), CH)
        return pltpu.make_async_copy(
            out.at[a, :, hid], (gw_hbm, uw_hbm)[a].at[:, hid], osem.at[i, a]
        )

    def finish(i):
        z_copy(i).wait_recv()
        tot = fin[i] + zr[i].astype(F32)
        hid = pl.ds(pl.multiple_of(i * CH, CH), CH)
        out[0, :, hid] = tot[:, :CH].astype(BF)
        out[1, :, hid] = tot[:, CH:].astype(BF)
        out_copy(i, 0).start()
        out_copy(i, 1).start()

    def weighed(j):
        return jnp.where(j < X0, 0, jnp.minimum(jnp.minimum(2 * (j - X0 + 1), j - 1), NC))

    @pl.loop(0, NC + 3)
    def _(j):
        @pl.when(j < NC)
        def _():
            grads(j, NA, NB)
            b_send(j, 0).start()
            b_send(j, 1).start()

        @pl.when(j == 0)
        def _():
            xg_landed(1, 2)
            xg_go(5, 6, 9, 10)

        @pl.when(jnp.logical_and(j >= 1, j < NC + 1))
        def _():
            b_pass(j - 1)

        @pl.when(j == 1)
        def _():
            xg_landed(3, 4)
            xg_go(7, 8)
            xg_landed(6)
            xg_go(11)

        @pl.when(j == X0 - 1)
        def _():
            build_xt()

        @pl.when(j == X0 + 3)
        def _():
            in_cov()

        @pl.when(j == X0 + 4)
        def _():
            ic_copy.wait_recv()
            zis[...] = ic[pl.ds(64, 32), :] + icr[pl.ds(0, 32), :]
            in_across.start()

        @pl.loop(weighed(j - 2), weighed(j - 1))
        def _(i):
            combine(i)

        @pl.loop(weighed(j - 1), weighed(j))
        def _(i):
            weigh(i)

        @pl.when(jnp.logical_and(j == BC + 2, x < 2))
        def _():
            cov()

        @pl.when(jnp.logical_and(j == BC + 3, x < 2))
        def _():
            cov_across()

        @pl.when(jnp.logical_and(j == NC + 1, x >= 2))
        def _():
            cov()

        @pl.when(jnp.logical_and(j == NC + 2, x >= 2))
        def _():
            cov_across()

        @pl.when(j >= ZLAG)
        def _():
            finish(j - ZLAG)

    in_across.wait()
    zis[...] = (ic[pl.ds(96, 32), :] + icr[pl.ds(32, 32), :] + zir[...]) * (1.0 / 4096.0)

    @pl.loop(NC + 3 - ZLAG, NC)
    def _(i):
        finish(i)

    zcov_copy.wait_recv()
    for a in range(2):
        ccr[zl, a] = own_cov(zl, a) + zcr[a].astype(F32)
    last = [
        pltpu.make_async_copy(zis, ic_hbm, loc.at[0]),
        pltpu.make_async_copy(ccr.at[zl, 0], gc_hbm, loc.at[1]),
        pltpu.make_async_copy(ccr.at[zl, 1], uc_hbm, loc.at[2]),
    ]
    for cp in last:
        cp.start()

    for dz, dy in peers:
        oa_copy(dz, dy).wait_send()
        spread(dz, dy).wait_send()
    for dx in (1, 2, 3):
        to_x(dx).wait_send()
    for i in range(12):
        ob_step(i).wait_send()
        xg_step(i).wait_send()

    @pl.loop(0, NC)
    def _(j):
        for way in range(2):
            a_send(j, way).wait_send()
            a_fwd(j, way).wait_send()
            b_send(j, way).wait_send()
            b_fwd(j, way).wait_send()
            out_copy(j, way).wait()
        z_copy(j).wait_send()

        @pl.when(j >= NC - KSLOTS)
        def _():
            k_copy(j).wait_send()

    ic_copy.wait_send()
    cov_copy(0).wait_send()
    cov_copy(1).wait_send()
    zcov_copy.wait_send()
    for cp in last:
        cp.wait()


def copy_all(*refs):
    ins, outs, held, sems = refs[:5], refs[5:10], refs[10:15], refs[15]
    first = [pltpu.make_async_copy(ins[i], held[i], sems.at[0, i]) for i in range(5)]
    then = [pltpu.make_async_copy(held[i], outs[i], sems.at[1, i]) for i in range(5)]
    for cp in first:
        cp.start()
    for a, b in zip(first, then):
        a.wait()
        b.start()
    for cp in then:
        cp.wait()


def on_device(inputs, gate_pre, up_pre, out_grad, down_weight):
    dma = pltpu.SemaphoreType.DMA
    vm = pltpu.VMEM
    shapes = (
        jax.ShapeDtypeStruct((TOK, H), BF),
        jax.ShapeDtypeStruct((TOK, H), BF),
        jax.ShapeDtypeStruct((32, DB), F32),
        jax.ShapeDtypeStruct((CR, HB), F32),
        jax.ShapeDtypeStruct((CR, HB), F32),
    )
    anywhere = pl.BlockSpec(memory_space=pl.ANY)
    outs = pl.pallas_call(
        kernel,
        out_shape=shapes,
        in_specs=[anywhere] * 5,
        out_specs=tuple([anywhere] * 5),
        scratch_shapes=[
            vm((TOK, D), BF),
            vm((H, D), BF),
            vm((TOK, H), BF),
            vm((TOK, H), BF),
            vm((NC, T4, CW), BF),
            vm((8, 32, DS), BF),
            vm((2, 4, 8, 32, DS), BF),
            vm((DB, T4), BF),
            vm((KSLOTS, DB, CW), F32),
            vm((KSLOTS, 512, CW), F32),
            vm((NC, TOK, CW), F32),
            vm((NC, TOK, CW), BF),
            vm((NC, TOK, CW), BF),
            vm((2, 512, T4), BF),
            vm((2, 512, HB), F32),
            vm((2, 2, CR, HB), F32),
            vm((2, CR, HB), BF),
            vm((2, CR, HB), BF),
            vm((128, DB), F32),
            vm((64, DB), F32),
            vm((32, DB), F32),
            vm((32, DB), F32),
            vm((2, TOK, H), BF),
            dma((5,)),
            dma((NC,)),
            dma((NC, 2)),
            dma((2, 4)), dma((2, 4)),
            dma((12,)), dma((12,)),
            dma((2, 4)), dma((2, 4)),
            dma((3,)), dma((3,)),
            dma((12,)), dma((12,)),
            dma((NC, 2)), dma((NC, 2)), dma((NC, 2)), dma((NC, 2)),
            dma((NC, 2)), dma((NC, 2)), dma((NC, 2)), dma((NC, 2)),
            dma((NC,)), dma((NC,)),
            dma((NC,)), dma((NC,)),
            dma((5,)), dma((5,)),
        ],
        compiler_params=pltpu.CompilerParams(
            collective_id=0, has_side_effects=True, vmem_limit_bytes=62 << 20
        ),
    )(inputs, gate_pre, up_pre, out_grad, down_weight)
    gw, uw, ic, gc, uc = pl.pallas_call(
        copy_all,
        out_shape=shapes,
        in_specs=[anywhere] * 5,
        out_specs=tuple([anywhere] * 5),
        scratch_shapes=[vm(a.shape, a.dtype) for a in shapes] + [dma((2, 5))],
    )(*outs)
    return gw, uw, ic, gc[None], uc[None]


def solution(mesh):
    placed = (
        P("dp", "tensor"),
        P("dp", "tensor"),
        P("dp", "tensor"),
        P("dp", "tensor"),
        P("tensor", None),
    )
    return jax.shard_map(
        on_device,
        mesh=mesh,
        in_specs=placed,
        out_specs=(
            P("dp", "tensor"),
            P("dp", "tensor"),
            P(("dp", "tensor"), None),
            P("tensor", "dp", None),
            P("tensor", "dp", None),
        ),
        check_vma=False,
    )
```

time: 152 us -> 123 us (0.81)
  Pallas kernels: 142 us -> 123 us
  local copies, waits for them, and re-layouts: 9.43 us -> 0 us
    pallas_call x1 -> x2, Pallas kernels: 142 us -> 123 us  [the longest x1 120 us: on_device(): pl.pallas_call(kernel, out_shape=shapes, in_specs=[anywhere] * 5, out_spe...]
    unnamed x5 -> x0, local copies, waits for them, and re-layouts: 9.43 us -> none
where the time goes in v2:
time: 123 us
  Pallas kernels  123 us (100%)
    pallas_call x1, Pallas kernels, on_device(): pl.pallas_call(kernel, out_shape=shapes, in_specs=[anywhere] * 5, out_spe...  120 us
    pallas_call x1, Pallas kernels, on_device(): pl.pallas_call(copy_all, out_shape=shapes, in_specs=[anywhere] * 5, out_s...  2.79 us

profile of v2, /device:TPU:7, one launch (start us, length us, event | category | flops | bytes accessed | tf_op | source)
XLA Modules:
  0.0 123.2 jit_solution(14553335193816186617)
XLA Ops:
  0.6 119.8 %shard_map.92 = (bf16[256,1792]{1,0:T(8,128)(2,1)}, bf16[256,1792]{1,0:T(8,128)(2,1)}, f32[32,1024]{1,0:T(8,128)}, f32[112,896]{1,0:T(8,128)}, f32[112,896]{1,0:T(8,128)}) custom-call(bf16[256,512]{1,0:T(8,128)(2,1)} %x_hbm.1, bf16[256,1792]{1,0:T(8,128)(2,1)} %gp_hbm.1, bf16[256,1792]{1,0:T(8,128)(2,1)} %up_hbm.1, bf16[256,512]{1,0:T(8,128)(2,1)} %og_hbm.1, ...), custom_call_target="tpu_custom_call" | custom-call | tf_op jit(solution)/shard_map/pallas_call | solution.py:537
  120.4 2.8 %shard_map.93 = (bf16[256,1792]{1,0:T(8,128)(2,1)}, bf16[256,1792]{1,0:T(8,128)(2,1)}, f32[32,1024]{1,0:T(8,128)}, f32[112,896]{1,0:T(8,128)}, f32[112,896]{1,0:T(8,128)}) custom-call(bf16[256,1792]{1,0:T(8,128)(2,1)} %get-tuple-element.15.refs_0_, bf16[256,1792]{1,0:T(8,128)(2,1)} %get-tuple-element.16.refs_1_, f32[32,1024]{1,0:T(8,128)} %get-tuple-element.17.refs_2_, ...), custom_call_target="tpu_custom_call" | custom-call | tf_op jit(solution)/shard_map/pallas_call | solution.py:584
